TPU v7x, 512 devices: a whole 4x8x8 slice. The times are simulated.
512 devices in a mesh: seq: 64 (over x, y, z_lo), tp: 8 (over z_hi, core).
Axes of the slice: x: 4, y: 8, z: 8 (z_hi: 4, z_lo: 2; z = z_hi * 2 + z_lo), core: 2. Of those that a mesh axis runs over, the one named last changes fastest.
Arguments:
- queries: bfloat16 [16384, 3072], P(('seq', 'tp')), may hold values from -42 to 42
- keys: bfloat16 [16384, 3072], P(('seq', 'tp')), may hold values from -6 to 6
- values: bfloat16 [16384, 3072], P(('seq', 'tp')), may hold values from -6 to 6
- pool_keys: bfloat16 [64, 128, 3072], P('seq', None, 'tp'), may hold values from -6 to 6
- pool_values: bfloat16 [64, 128, 3072], P('seq', None, 'tp'), may hold values from -6 to 6
- page_table: int32 [64], replicated, may hold values from 0 to 63, each once
- lengths: int32 [128], replicated, may hold values from 1 to 256, 16384 in all
- group_of: int32 [128], replicated, may hold values from 0 to 1
Outputs:
- context: bfloat16 [16384, 3072], P(('seq', 'tp'))
- new_keys: bfloat16 [16384, 3072], P('seq', 'tp')
- new_values: bfloat16 [16384, 3072], P('seq', 'tp')
Inputs may be any that keep to these rules, and one draw needn't show every extreme that they name: `page_table`: each of the 64 slots appears once; entries g * 32 to (g + 1) * 32 - 1 are group g's pages; slot s lies on index s of seq. The lengths sum to 16384; each request's suffix tokens follow those of the requests before it.
All inputs are finite; a program needn't handle non-finite values.
Results may differ from a plain program's by a relative error of at most 0.0055.
Values may be sent and summed in bfloat16 or wider, within the bound.
A program may use at most 64 MiB of HBM per device.

v0:
```python
import math
import jax
import jax.numpy as jnp
from jax import lax
from jax.sharding import PartitionSpec as P

HD = 96
ROT = 24


def shifted(block, axis, distance):
    devices = range(lax.axis_size(axis))
    route = [(i - distance, i) for i in devices if i - distance in devices]
    return lax.ppermute(block, axis, route)


def rotate(matrix, position):
    count = matrix.shape[0]
    split_heads = matrix.reshape(count, -1, HD)
    half_rot = ROT // 2
    inverse_freq = 10000.0 ** (-(jnp.arange(half_rot, dtype=jnp.float32) * 2.0 / ROT))
    angles = position.astype(jnp.float32)[:, None] * inverse_freq[None, :]
    cosine = jnp.cos(angles)[:, None, :]
    sine = jnp.sin(angles)[:, None, :]
    first_half = split_heads[..., :half_rot]
    second_half = split_heads[..., half_rot:ROT]
    rest_dims = split_heads[..., ROT:]
    turned = jnp.concatenate(
        [
            first_half * cosine - second_half * sine,
            second_half * cosine + first_half * sine,
            rest_dims,
        ],
        axis=-1,
    )
    return turned.reshape(count, -1)


def local(queries, keys, values, pool_keys, pool_values, page_table, lengths, group_of):
    seq_count = lax.axis_size("seq")
    head_queries, head_keys, head_values = (
        lax.all_to_all(queries, "tp", split_axis=1, concat_axis=0, tiled=True),
        lax.all_to_all(keys, "tp", split_axis=1, concat_axis=0, tiled=True),
        lax.all_to_all(values, "tp", split_axis=1, concat_axis=0, tiled=True),
    )
    tok_rows = head_queries.shape[0]
    channels = head_queries.shape[1]
    heads_here = channels // HD
    page_rows = pool_keys.shape[1]
    slots_here = pool_keys.shape[0]
    slot_count = slots_here * seq_count
    pages_group = slot_count // 2
    prefix_len = pages_group * page_rows
    request_count = lengths.shape[0]
    request_ends = jnp.cumsum(lengths)
    request_starts = request_ends - lengths
    request_ids = jnp.arange(request_count, dtype=jnp.int32)
    my_index = lax.axis_index("seq")
    row_base = my_index * tok_rows
    query_rows = row_base + jnp.arange(tok_rows, dtype=jnp.int32)
    request = jnp.sum((query_rows[:, None] >= request_ends[None, :]).astype(jnp.int32), axis=1)
    one_hot = (request[:, None] == request_ids[None, :]).astype(jnp.int32)
    offset = query_rows - jnp.sum(one_hot * request_starts[None, :], axis=1)
    group = jnp.sum(one_hot * group_of[None, :], axis=1)
    position = prefix_len + offset
    rot_queries = rotate(head_queries.astype(jnp.float32), position).astype(jnp.bfloat16)
    rot_keys = rotate(head_keys.astype(jnp.float32), position).astype(jnp.bfloat16)
    earlier_keys, earlier_values = shifted((rot_keys, head_values), "seq", 1)
    earlier_rows = query_rows - tok_rows
    earlier_request = jnp.sum(
        (earlier_rows[:, None] >= request_ends[None, :]).astype(jnp.int32), axis=1
    )
    suffix_keys = jnp.concatenate([earlier_keys, rot_keys], axis=0)
    suffix_values = jnp.concatenate([earlier_values, head_values], axis=0)
    key_rows = jnp.concatenate([earlier_rows, query_rows], axis=0)
    key_request = jnp.concatenate([earlier_request, request], axis=0)
    suffix_mask = (
        (key_request[None, :] == request[:, None])
        & (key_rows[None, :] <= query_rows[:, None])
        & (key_rows[None, :] >= 0)
    )
    slot_ids = jnp.arange(slot_count, dtype=jnp.int32)
    member = (page_table[None, :] == slot_ids[:, None]) & (slot_ids[None, :] >= pages_group)
    slot_group = jnp.any(member, axis=1).astype(jnp.int32)
    score_scale = HD ** (-0.5)

    def attend(state, query_block, key_block, value_block, allowed):
        row_max, total, accum = state
        query_heads = query_block.reshape(query_block.shape[0], heads_here, HD)
        key_heads = key_block.reshape(key_block.shape[0], heads_here, HD)
        value_heads = value_block.reshape(value_block.shape[0], heads_here, HD)
        scores = (
            jnp.einsum("qhd,khd->hqk", query_heads, key_heads, preferred_element_type=jnp.float32)
            * score_scale
        )
        scores = jnp.where(allowed[None], scores, -1e30)
        new_max = jnp.maximum(row_max, jnp.max(scores, axis=-1))
        weights = jnp.where(allowed[None], jnp.exp(scores - new_max[..., None]), 0.0)
        factor = jnp.exp(row_max - new_max)
        new_total = total * factor + jnp.sum(weights, axis=-1)
        weights_bf16 = weights.astype(jnp.bfloat16)
        new_accum = accum * factor[..., None] + jnp.einsum(
            "hqk,khd->hqd", weights_bf16, value_heads, preferred_element_type=jnp.float32
        )
        return (new_max, new_total, new_accum)

    initial = (
        jnp.full((heads_here, tok_rows), -1e30, jnp.float32),
        jnp.zeros((heads_here, tok_rows), jnp.float32),
        jnp.zeros((heads_here, tok_rows, HD), jnp.float32),
    )
    state = initial
    piece_keys = lax.all_gather(pool_keys, "seq", axis=0, tiled=True)
    piece_slots = piece_keys.shape[0]
    piece_ids = jnp.arange(piece_slots, dtype=jnp.int32)
    piece_group = jnp.sum(
        (piece_ids[:, None] == slot_ids[None, :]).astype(jnp.int32) * slot_group[None, :], axis=1
    )
    block_pages = math.gcd(piece_slots, 4)
    block_count = piece_slots // block_pages
    keys_blocked = piece_keys.reshape(block_count, block_pages * page_rows, channels)
    values_blocked = lax.all_gather(pool_values, "seq", axis=0, tiled=True).reshape(
        block_count, block_pages * page_rows, channels
    )
    groups_blocked = piece_group.reshape(block_count, block_pages)

    def one_step(running, item):
        key_block, value_block, group_block = item
        key_group = jnp.repeat(group_block, page_rows)
        allowed = group[:, None] == key_group[None, :]
        return (attend(running, rot_queries, key_block, value_block, allowed), None)

    state, _ = lax.scan(one_step, state, (keys_blocked, values_blocked, groups_blocked))
    state = attend(state, rot_queries, suffix_keys, suffix_values, suffix_mask)
    final_max, final_total, final_accum = state
    context_heads = (
        (final_accum / final_total[..., None])
        .transpose(1, 0, 2)
        .reshape(tok_rows, channels)
        .astype(jnp.bfloat16)
    )
    context = lax.all_to_all(context_heads, "tp", split_axis=0, concat_axis=1, tiled=True)
    return (context, rot_keys, head_values)


def solution(mesh):
    return jax.shard_map(
        local,
        mesh=mesh,
        in_specs=(
            P(("seq", "tp"), None),
            P(("seq", "tp"), None),
            P(("seq", "tp"), None),
            P("seq", None, "tp"),
            P("seq", None, "tp"),
            P(),
            P(),
            P(),
        ),
        out_specs=(P(("seq", "tp"), None), P("seq", "tp"), P("seq", "tp")),
        check_vma=False,
    )
```

profile of v0, /device:TPU:1, one launch (start us, length us, event | category | flops | bytes accessed | tf_op | source)
XLA Modules:
  0.0 726.4 jit_solution(3364903707367896653)
XLA Ops:
  8.7 1.6 copy.109
  10.3 11.8 %all-to-all-start = ((bf16[32,8,384]{2,0,1:T(8,128)(2,1)}), bf16[32,8,384]{2,0,1:T(8,128)(2,1)S(1)}, u32[]{:S(2)}, u32[]{:S(2)}) async-start(bf16[32,8,384]{2,0,1:T(8,128)(2,1)} %bitcast.52), calls=%async_computation | async-start | bytes 393216 | tf_op jit(solution)/shard_map/all_to_all | solution.py:42
  25.0 1.6 copy.108
  27.5 4.6 all-to-all-done
  32.1 4.6 all-to-all-start.1
  37.7 12.3 %all-to-all-done.1 = bf16[32,8,384]{2,0,1:T(8,128)(2,1)S(1)} async-done(((bf16[32,8,384]{2,0,1:T(8,128)(2,1)}), bf16[32,8,384]{2,0,1:T(8,128)(2,1)S(1)}, u32[]{:S(2)}, u32[]{:S(2)}) %all-to-all-start.1) | async-done | bytes 196640 | tf_op jit(solution)/shard_map/all_to_all | solution.py:43
  50.0 3.7 all-to-all-start.2
  54.8 9.4 %all-to-all-done.2 = bf16[32,8,384]{2,0,1:T(8,128)(2,1)S(1)} async-done(((bf16[32,8,384]{2,0,1:T(8,128)(2,1)}), bf16[32,8,384]{2,0,1:T(8,128)(2,1)S(1)}, u32[]{:S(2)}, u32[]{:S(2)}) %all-to-all-start.2) | async-done | bytes 196640 | tf_op jit(solution)/shard_map/all_to_all | solution.py:44
  64.3 3.8 collective-permute-start.1
  69.3 3.3 collective-permute-start
  74.4 5.3 collective-permute-done
  79.7 1.9 fusion.13
  81.7 207.7 %all-gather.3.cloned.1.call-done = bf16[64,128,384]{2,1,0:T(8,128)(2,1)} async-done(((bf16[1,128,384]{2,1,0:T(8,128)(2,1)}), bf16[64,128,384]{2,1,0:T(8,128)(2,1)}) %all-gather.3.cloned.1.call-update) | async-done | bytes 6291472 | tf_op jit(solution)/shard_map/all_gather | solution.py:113
  289.4 305.0 %all-gather.5.cloned.1.call-done = bf16[64,128,384]{2,1,0:T(8,128)(2,1)} async-done(((bf16[1,128,384]{2,1,0:T(8,128)(2,1)}), bf16[64,128,384]{2,1,0:T(8,128)(2,1)}) %all-gather.5.cloned.1.call-update) | async-done | bytes 6291472 | tf_op jit(solution)/shard_map/all_gather | solution.py:122
  594.4 59.1 %while.15 = (s32[]{:T(128)}, f32[4,256]{1,0:T(4,128)S(1)}, f32[4,256]{1,0:T(4,128)S(1)}, f32[4,256,96]{1,2,0:T(8,128)S(1)}, s32[256]{0:T(256)S(1)}, /*index=5*/s...) while((s32[]{:T(128)}, f32[4,256]{1,0:T(4,128)S(1)}, ...), condition=%wide.region_9.10_spmd.clone, body=%wide.region_6.0_spmd.clone.sunk | while | flops 208573440 | bytes 11801785 | solution.py:133
  594.6 1.2 constant_dynamic-slice_fusion.4
  598.3 1.2 constant_dynamic-slice_fusion.4
  602.0 1.2 constant_dynamic-slice_fusion.4
  605.7 1.2 constant_dynamic-slice_fusion.4
  609.4 1.2 constant_dynamic-slice_fusion.4
  613.1 1.2 constant_dynamic-slice_fusion.4
  653.6 2.5 fusion.14
  658.0 50.2 %all-to-all-start.3 = ((bf16[8,32,384]{2,1,0:T(8,128)(2,1)}), bf16[8,32,384]{2,1,0:T(8,128)(2,1)S(1)}, u32[]{:S(2)}, u32[]{:S(2)}) async-start(bf16[8,32,384]{2,1,0:T(8,128)(2,1)} %convert_element_type.86), calls=%async_computation.3 | async-start | bytes 393216 | tf_op jit(solution)/shard_map/all_to_all | solution.py:142
  708.9 9.2 %all-to-all-done.3 = bf16[8,32,384]{2,1,0:T(8,128)(2,1)S(1)} async-done(((bf16[8,32,384]{2,1,0:T(8,128)(2,1)}), bf16[8,32,384]{2,1,0:T(8,128)(2,1)S(1)}, u32[]{:S(2)}, u32[]{:S(2)}) %all-to-all-start.3) | async-done | bytes 196640 | tf_op jit(solution)/shard_map/all_to_all | solution.py:142
  (248 shorter events, 65.0 us)
Async XLA Ops:
  7.2 29.6 %copy-start.1 = (bf16[32,3072]{1,0:T(8,128)(2,1)S(1)}, bf16[32,3072]{1,0:T(8,128)(2,1)}, u32[]{:S(2)}) copy-start(bf16[32,3072]{1,0:T(8,128)(2,1)} %param.12) | copy-start | bytes 589828
  7.2 282.2 %all-gather.3.cloned.1.call-start = ((), (), s32[]{:S(2)}) async-start(), calls=%async_computation.4 | async-start | bytes 6389760 | tf_op jit(solution)/shard_map/all_gather | solution.py:113
  7.9 586.5 %all-gather.5.cloned.1.call-start = ((), (), s32[]{:S(2)}) async-start(), calls=%async_computation.5 | async-start | bytes 6389760 | tf_op jit(solution)/shard_map/all_gather | solution.py:122
  10.3 21.8 %all-to-all-start = ((bf16[32,8,384]{2,0,1:T(8,128)(2,1)}), bf16[32,8,384]{2,0,1:T(8,128)(2,1)S(1)}, u32[]{:S(2)}, u32[]{:S(2)}) async-start(bf16[32,8,384]{2,0,1:T(8,128)(2,1)} %bitcast.52), calls=%async_computation | async-start | bytes 393216 | tf_op jit(solution)/shard_map/all_to_all | solution.py:42
  32.1 17.9 %all-to-all-start.1 = ((bf16[32,8,384]{2,0,1:T(8,128)(2,1)}), bf16[32,8,384]{2,0,1:T(8,128)(2,1)S(1)}, u32[]{:S(2)}, u32[]{:S(2)}) async-start(bf16[32,8,384]{2,0,1:T(8,128)(2,1)} %bitcast.51), calls=%async_computation.1 | async-start | bytes 393216 | tf_op jit(solution)/shard_map/all_to_all | solution.py:43
  50.0 14.3 %all-to-all-start.2 = ((bf16[32,8,384]{2,0,1:T(8,128)(2,1)}), bf16[32,8,384]{2,0,1:T(8,128)(2,1)S(1)}, u32[]{:S(2)}, u32[]{:S(2)}) async-start(bf16[32,8,384]{2,0,1:T(8,128)(2,1)} %bitcast.50), calls=%async_computation.2 | async-start | bytes 393216 | tf_op jit(solution)/shard_map/all_to_all | solution.py:44
  64.3 9.9 %collective-permute-start.1 = (bf16[256,384]{1,0:T(8,128)(2,1)S(1)}, bf16[256,384]{1,0:T(8,128)(2,1)S(1)}, u32[]{:S(2)}, u32[]{:S(2)}) collective-permute-start(bf16[256,384]{1,0:T(8,128)(2,1)S(1)} %bitcast.79), channel_id=1, source_target_pairs={{0,8},{8,16},{16,24},{24,32},{32,40},{40,48},{48,56},{56,64},{64,7... | collective-permute-start | bytes 589832 | tf_op jit(solution)/shard_map/ppermute | solution.py:14
  69.3 10.4 %collective-permute-start = (bf16[256,384]{0,1:T(8,128)(2,1)S(1)}, bf16[256,384]{0,1:T(8,128)(2,1)S(1)}, u32[]{:S(2)}, u32[]{:S(2)}) collective-permute-start(bf16[256,384]{0,1:T(8,128)(2,1)S(1)} %bitcast.82), channel_id=1, source_target_pairs={{0,8},{8,16},{16,24},{24,32},{32,40},{40,48},{48,56},{56,64},{64,7... | collective-permute-start | bytes 589832 | tf_op jit(solution)/shard_map/ppermute | solution.py:14
  653.5 2.6 copy-start
  658.0 60.2 %all-to-all-start.3 = ((bf16[8,32,384]{2,1,0:T(8,128)(2,1)}), bf16[8,32,384]{2,1,0:T(8,128)(2,1)S(1)}, u32[]{:S(2)}, u32[]{:S(2)}) async-start(bf16[8,32,384]{2,1,0:T(8,128)(2,1)} %convert_element_type.86), calls=%async_computation.3 | async-start | bytes 393216 | tf_op jit(solution)/shard_map/all_to_all | solution.py:142
Sparse Core Ops, SparseCore 0:
  10.1 279.2 all-gather.2
  291.5 302.8 all-gather.4
where the time goes:
time: 727 us; the launch traced here: 726 us
  waiting for transfers between devices  555 us (76%)
  starting transfers between devices  77.5 us (11%)
  local copies, waits for them, and re-layouts  37.7 us (5%)
  matrix products  22.9 us (3%)
  other arithmetic  17.8 us (2%)
  between operations  14.3 us (2%)
    all_gather x1, waiting for transfers between devices, local(): lax.all_gather(pool_values, 'seq', axis=0, tiled=True)  305 us
    all_gather x1, waiting for transfers between devices, local(): piece_keys = lax.all_gather(pool_keys, 'seq', axis=0, tiled=True)  208 us
    all_to_all x1, starting transfers between devices, local(): lax.all_to_all(context_heads, 'tp', split_axis=0, concat_axis=1, tiled=True)  50.2 us
    dynamic_slice x48, local copies, waits for them, and re-layouts, local(): lax.scan(one_step, state, (keys_blocked, values_blocked, groups_blocked))  25.3 us
  transfers between devices with their start and end apart: 8, of which 7 were waited for; matrix products, arithmetic and copies ran while one was open for 2% of the time, Pallas kernels for 0%

commit v1 on v0

--- a/solution.py
+++ b/solution.py
@@ -110,7 +110,9 @@
         jnp.zeros((heads_here, tok_rows, HD), jnp.float32),
     )
     state = initial
-    piece_keys = lax.all_gather(pool_keys, "seq", axis=0, tiled=True)
+    piece_keys = jnp.concatenate(
+        lax.all_to_all(jnp.stack([pool_keys] * lax.axis_size("seq")), "seq", 0, 0), axis=0
+    )
     piece_slots = piece_keys.shape[0]
     piece_ids = jnp.arange(piece_slots, dtype=jnp.int32)
     piece_group = jnp.sum(

time: 727 us -> 564 us (0.78)
  waiting for transfers between devices: 555 us -> 322 us
  matrix products: 22.9 us -> 51.3 us
  local copies, waits for them, and re-layouts: 37.7 us -> 53.8 us
  blocking collectives: 0 us -> 13.1 us
  other arithmetic: 17.8 us -> 27.4 us
    all_gather x1 -> x0, waiting for transfers between devices: 208 us -> none  [local(): piece_keys = lax.all_gather(pool_keys, 'seq', axis=0, tiled=True)]
    all_gather x1, waiting for transfers between devices: 305 us -> 147 us  [local(): lax.all_gather(pool_values, 'seq', axis=0, tiled=True)]
    all_to_all x1, waiting for transfers between devices: 9.43 us -> 128 us  [local(): lax.all_to_all(jnp.stack([pool_keys] * lax.axis_size('seq')), 'seq', 0, 0)]
    dot_general x17, matrix products: 12.1 us -> 39.9 us  [attend(): jnp.einsum('hqk,khd->hqd', weights_bf16, value_heads, preferred_element_t...]
    ppermute x2, waiting for transfers between devices: 5.34 us -> 22.5 us  [shifted(): return lax.ppermute(block, axis, route)]
    all_to_all x0 -> x1, blocking collectives: none -> 13.1 us  [local(): lax.all_to_all(values, 'tp', split_axis=1, concat_axis=0, tiled=True)]
    squeeze x16, local copies, waits for them, and re-layouts: 0.15 us -> 10.8 us  [local(): lax.scan(one_step, state, (keys_blocked, values_blocked, groups_blocked))]
    eq x16, other arithmetic: 2.29 us -> 12.7 us  [one_step(): allowed = group[:, None] == key_group[None, :]]
  transfers between devices with their start and end apart: 8 -> 7, of which waited for: 7 -> 6; matrix products, arithmetic and copies ran while one was open for 2% -> 2% of each run, Pallas kernels for 0% -> 0%
where the time goes in v1:
time: 564 us; the launch traced here: 562 us
  waiting for transfers between devices  322 us (57%)
  starting transfers between devices  78.7 us (14%)
  local copies, waits for them, and re-layouts  53.8 us (10%)
  matrix products  51.3 us (9%)
  other arithmetic  27.4 us (5%)
  between operations  14.3 us (3%)
  blocking collectives  13.1 us (2%)
    all_gather x1, waiting for transfers between devices, local(): lax.all_gather(pool_values, 'seq', axis=0, tiled=True)  147 us
    all_to_all x1, waiting for transfers between devices, local(): lax.all_to_all(jnp.stack([pool_keys] * lax.axis_size('seq')), 'seq', 0, 0)  128 us
    all_to_all x1, starting transfers between devices, local(): lax.all_to_all(context_heads, 'tp', split_axis=0, concat_axis=1, tiled=True)  44.3 us
    dot_general x17, matrix products, attend(): jnp.einsum('hqk,khd->hqd', weights_bf16, value_heads, preferred_element_t...  39.9 us
    dynamic_slice x48, local copies, waits for them, and re-layouts, local(): lax.scan(one_step, state, (keys_blocked, values_blocked, groups_blocked))  25.4 us
    ppermute x2, waiting for transfers between devices, shifted(): return lax.ppermute(block, axis, route)  22.5 us
    all_to_all x1, blocking collectives, local(): lax.all_to_all(values, 'tp', split_axis=1, concat_axis=0, tiled=True)  13.1 us
    eq x16, other arithmetic, one_step(): allowed = group[:, None] == key_group[None, :]  12.7 us
  transfers between devices with their start and end apart: 7, of which 6 were waited for; matrix products, arithmetic and copies ran while one was open for 2% of the time, Pallas kernels for 0%

profile of v1, /device:TPU:1, one launch (start us, length us, event | category | flops | bytes accessed | tf_op | source)
XLA Modules:
  0.0 561.6 jit_solution(2506320380217209732)
XLA Ops:
  8.8 11.8 %all-to-all-start.2 = ((bf16[32,8,384]{2,0,1:T(8,128)(2,1)}), bf16[32,8,384]{2,0,1:T(8,128)(2,1)S(1)}, u32[]{:S(2)}, u32[]{:S(2)}) async-start(bf16[32,8,384]{2,0,1:T(8,128)(2,1)} %bitcast.52), calls=%async_computation.2 | async-start | bytes 393216 | tf_op jit(solution)/shard_map/all_to_all | solution.py:43
  22.2 8.4 %all-to-all-done.2 = bf16[32,8,384]{2,0,1:T(8,128)(2,1)S(1)} async-done(((bf16[32,8,384]{2,0,1:T(8,128)(2,1)}), bf16[32,8,384]{2,0,1:T(8,128)(2,1)S(1)}, u32[]{:S(2)}, u32[]{:S(2)}) %all-to-all-start.2) | async-done | bytes 196640 | tf_op jit(solution)/shard_map/all_to_all | solution.py:43
  30.6 4.6 all-to-all-start.1
  36.2 7.7 %all-to-all-done.1 = bf16[32,8,384]{2,0,1:T(8,128)(2,1)S(1)} async-done(((bf16[32,8,384]{2,0,1:T(8,128)(2,1)}), bf16[32,8,384]{2,0,1:T(8,128)(2,1)S(1)}, u32[]{:S(2)}, u32[]{:S(2)}) %all-to-all-start.1) | async-done | bytes 196640 | tf_op jit(solution)/shard_map/all_to_all | solution.py:42
  43.9 13.1 %all_to_all.66 = bf16[32,8,384]{2,0,1:T(8,128)(2,1)S(1)} all-to-all(bf16[32,8,384]{2,0,1:T(8,128)(2,1)S(1)} %bitcast.89), channel_id=1, replica_groups=mesh['seq'=64,'tp'=8] {'tp'}, dimensions={1} | all-to-all | bytes 393216 | tf_op jit(solution)/shard_map/all_to_all | solution.py:44
  57.0 3.6 stack.2
  60.6 12.0 %all-to-all-start = ((bf16[64,1,128,384]{3,2,1,0:T(8,128)(2,1)}), bf16[64,1,128,384]{3,2,1,0:T(8,128)(2,1)}, u32[]{:S(2)}, u32[]{:S(2)}) async-start(bf16[64,1,128,384]{3,2,1,0:T(8,128)(2,1)} %stack.2), calls=%async_computation | async-start | bytes 12582912 | tf_op jit(solution)/shard_map/all_to_all | solution.py:114
  78.0 2.9 collective-permute-start
  82.0 3.1 collective-permute-start.1
  86.6 22.5 %collective-permute-done.1 = bf16[256,384]{1,0:T(8,128)(2,1)S(1)} collective-permute-done((bf16[256,384]{1,0:T(8,128)(2,1)S(1)}, bf16[256,384]{1,0:T(8,128)(2,1)S(1)}, u32[]{:S(2)}, u32[]{:S(2)}) %collective-permute-start.1) | collective-permute-done | bytes 196640 | tf_op jit(solution)/shard_map/ppermute | solution.py:14
  110.0 2.5 fusion.13
  112.5 128.2 %all-to-all-done = bf16[64,1,128,384]{3,2,1,0:T(8,128)(2,1)} async-done(((bf16[64,1,128,384]{3,2,1,0:T(8,128)(2,1)}), bf16[64,1,128,384]{3,2,1,0:T(8,128)(2,1)}, u32[]{:S(2)}, u32[]{:S(2)}) %all-to-all-start) | async-done | bytes 6291488 | tf_op jit(solution)/shard_map/all_to_all | solution.py:114
  240.6 146.9 %all-gather.2.cloned.1.call-done = bf16[64,128,384]{2,1,0:T(8,128)(2,1)} async-done(((bf16[1,128,384]{2,1,0:T(8,128)(2,1)}), bf16[64,128,384]{2,1,0:T(8,128)(2,1)}) %all-gather.2.cloned.1.call-update) | async-done | bytes 6291472 | tf_op jit(solution)/shard_map/all_gather | solution.py:124
  387.6 106.5 %while.15 = (s32[]{:T(128)}, f32[4,256]{1,0:T(4,128)S(1)}, f32[4,256]{1,0:T(4,128)S(1)}, f32[4,256,96]{1,2,0:T(8,128)}, s32[256]{0:T(256)}, /*index=5*/s32[16,4]...) while((s32[]{:T(128)}, f32[4,256]{1,0:T(4,128)S(1)}, ...), condition=%wide.region_9.10_spmd.clone, body=%wide.region_6.0_spmd.clone.sunk | while | flops 208573440 | bytes 11801777 | solution.py:135
  397.6 2.4 convolution_add_fusion.3
  411.0 2.4 convolution_add_fusion.3
  424.5 2.4 convolution_add_fusion.3
  437.9 2.4 convolution_add_fusion.3
  444.6 2.4 convolution_add_fusion.3
  451.4 2.4 convolution_add_fusion.3
  458.1 2.4 convolution_add_fusion.3
  464.8 2.4 convolution_add_fusion.3
  500.4 44.3 %all-to-all-start.4 = ((bf16[8,32,384]{2,1,0:T(8,128)(2,1)}), bf16[8,32,384]{2,1,0:T(8,128)(2,1)S(1)}, u32[]{:S(2)}, u32[]{:S(2)}) async-start(bf16[8,32,384]{2,1,0:T(8,128)(2,1)} %convert_element_type.86), calls=%async_computation.4 | async-start | bytes 393216 | tf_op jit(solution)/shard_map/all_to_all | solution.py:144
  545.6 7.8 %all-to-all-done.4 = bf16[8,32,384]{2,1,0:T(8,128)(2,1)S(1)} async-done(((bf16[8,32,384]{2,1,0:T(8,128)(2,1)}), bf16[8,32,384]{2,1,0:T(8,128)(2,1)S(1)}, u32[]{:S(2)}, u32[]{:S(2)}) %all-to-all-start.4) | async-done | bytes 196640 | tf_op jit(solution)/shard_map/all_to_all | solution.py:144
  (257 shorter events, 107.7 us)
Async XLA Ops:
  7.2 49.8 %copy-start.3 = (bf16[1,128,384]{2,1,0:T(8,128)(2,1)S(1)}, bf16[1,128,384]{2,1,0:T(8,128)(2,1)}, u32[]{:S(2)}) copy-start(bf16[1,128,384]{2,1,0:T(8,128)(2,1)} %param.13) | copy-start | bytes 294916
  8.8 21.8 %all-to-all-start.2 = ((bf16[32,8,384]{2,0,1:T(8,128)(2,1)}), bf16[32,8,384]{2,0,1:T(8,128)(2,1)S(1)}, u32[]{:S(2)}, u32[]{:S(2)}) async-start(bf16[32,8,384]{2,0,1:T(8,128)(2,1)} %bitcast.52), calls=%async_computation.2 | async-start | bytes 393216 | tf_op jit(solution)/shard_map/all_to_all | solution.py:43
  30.6 13.3 %all-to-all-start.1 = ((bf16[32,8,384]{2,0,1:T(8,128)(2,1)}), bf16[32,8,384]{2,0,1:T(8,128)(2,1)S(1)}, u32[]{:S(2)}, u32[]{:S(2)}) async-start(bf16[32,8,384]{2,0,1:T(8,128)(2,1)} %bitcast.53), calls=%async_computation.1 | async-start | bytes 393216 | tf_op jit(solution)/shard_map/all_to_all | solution.py:42
  60.6 12.8 %copy-start.4 = (s32[128]{0:T(128)S(1)}, s32[128]{0:T(128)}, u32[]{:S(2)}) copy-start(s32[128]{0:T(128)} %param.16) | copy-start | bytes 1540
  60.6 13.3 %copy-start.6 = (s32[64]{0:T(128)S(1)}, s32[64]{0:T(128)}, u32[]{:S(2)}) copy-start(s32[64]{0:T(128)} %param.15) | copy-start | bytes 772
  60.6 14.5 %copy-start.5 = (s32[128]{0:T(128)S(1)}, s32[128]{0:T(128)}, u32[]{:S(2)}) copy-start(s32[128]{0:T(128)} %param.17) | copy-start | bytes 1540
  60.6 180.0 %all-to-all-start = ((bf16[64,1,128,384]{3,2,1,0:T(8,128)(2,1)}), bf16[64,1,128,384]{3,2,1,0:T(8,128)(2,1)}, u32[]{:S(2)}, u32[]{:S(2)}) async-start(bf16[64,1,128,384]{3,2,1,0:T(8,128)(2,1)} %stack.2), calls=%async_computation | async-start | bytes 12582912 | tf_op jit(solution)/shard_map/all_to_all | solution.py:114
  72.6 314.9 %all-gather.2.cloned.1.call-start = ((), (), s32[]{:S(2)}) async-start(), calls=%async_computation.5 | async-start | bytes 6389760 | tf_op jit(solution)/shard_map/all_gather | solution.py:124
  78.0 31.9 %copy-start.1 = (bf16[256,4,96]{0,2,1:T(8,128)(2,1)}, bf16[256,4,96]{0,2,1:T(8,128)(2,1)S(1)}, u32[]{:S(2)}) copy-start(bf16[256,4,96]{0,2,1:T(8,128)(2,1)S(1)} %copy.87) | copy-start | bytes 589828
  78.0 31.9 %collective-permute-start = (bf16[256,384]{0,1:T(8,128)(2,1)S(1)}, bf16[256,384]{0,1:T(8,128)(2,1)S(1)}, u32[]{:S(2)}, u32[]{:S(2)}) collective-permute-start(bf16[256,384]{0,1:T(8,128)(2,1)S(1)} %bitcast.83), channel_id=1, source_target_pairs={{0,8},{8,16},{16,24},{24,32},{32,40},{40,48},{48,56},{56,64},{64,7... | collective-permute-start | bytes 589832 | tf_op jit(solution)/shard_map/ppermute | solution.py:14
  82.0 27.1 %collective-permute-start.1 = (bf16[256,384]{1,0:T(8,128)(2,1)S(1)}, bf16[256,384]{1,0:T(8,128)(2,1)S(1)}, u32[]{:S(2)}, u32[]{:S(2)}) collective-permute-start(bf16[256,384]{1,0:T(8,128)(2,1)S(1)} %bitcast.80), channel_id=1, source_target_pairs={{0,8},{8,16},{16,24},{24,32},{32,40},{40,48},{48,56},{56,64},{64,7... | collective-permute-start | bytes 589832 | tf_op jit(solution)/shard_map/ppermute | solution.py:14
  494.1 3.2 copy-start
  497.4 47.4 %copy-start.2 = (bf16[256,4,96]{0,2,1:T(8,128)(2,1)S(1)}, bf16[256,4,96]{0,2,1:T(8,128)(2,1)}, u32[]{:S(2)}) copy-start(bf16[256,4,96]{0,2,1:T(8,128)(2,1)} %copy-done.1) | copy-start | bytes 589828
  500.4 52.9 %all-to-all-start.4 = ((bf16[8,32,384]{2,1,0:T(8,128)(2,1)}), bf16[8,32,384]{2,1,0:T(8,128)(2,1)S(1)}, u32[]{:S(2)}, u32[]{:S(2)}) async-start(bf16[8,32,384]{2,1,0:T(8,128)(2,1)} %convert_element_type.86), calls=%async_computation.4 | async-start | bytes 393216 | tf_op jit(solution)/shard_map/all_to_all | solution.py:144
Sparse Core Ops, SparseCore 0:
  75.5 312.0 all-gather.1
